TPU v7x, 32 devices: a whole 2x2x4 slice. The times are simulated.
32 devices in a mesh: expert: 4 (over z), fsdp: 8 (over y, x, core).
Axes of the slice: x: 2, y: 2, z: 4, core: 2. Of those that a mesh axis runs over, the one named last changes fastest.
Arguments:
- tokens: bfloat16 [8192, 2048], P(('expert', 'fsdp')), may hold values from -6 to 6
- expert_ids: int32 [8192, 6], P(('expert', 'fsdp')), may hold values from 0 to 63, as said below
- gate_vals: bfloat16 [8192, 6], P(('expert', 'fsdp')), may hold values from 0.099609375 to 1
- w_gate: bfloat16 [4, 2048, 1408], P('expert', 'fsdp'), may hold values from -0.125 to 0.125
- w_up: bfloat16 [4, 2048, 1408], P('expert', 'fsdp'), may hold values from -0.125 to 0.125
- w_down: bfloat16 [4, 2048, 1408], P('expert', 'fsdp'), may hold values from -0.15625 to 0.15625
- cotangent: bfloat16 [8192, 2048], P(('expert', 'fsdp')), may hold values from -6 to 6
Outputs:
- output: bfloat16 [8192, 2048], P(('expert', 'fsdp'))
- grad_tokens: bfloat16 [8192, 2048], P(('expert', 'fsdp'))
- grad_gates: float32 [8192, 6], P(('expert', 'fsdp'))
- grad_w_gate: float32 [4, 2048, 1408], P('expert', 'fsdp')
- grad_w_up: float32 [4, 2048, 1408], P('expert', 'fsdp')
- grad_w_down: float32 [4, 2048, 1408], P('expert', 'fsdp')
Inputs may be any that keep to these rules, and one draw needn't show every extreme that they name: `expert_ids`: each row names 6 different experts. Among the tokens of one device at most 48 name any one expert whose number modulo 16 is below 1. On every device some such expert is named by exactly 48 of its tokens, and for every column one such expert is named by exactly 48 tokens of every device of that column.
All inputs are finite; a program needn't handle non-finite values.
Results may differ from a plain program's by a relative error of at most 0.013.
Values may be sent and summed in bfloat16 or wider, within the bound.
A program may use at most 128 MiB of HBM per device.

v0:
```python
import functools

import jax
import jax.numpy as jnp
from jax import lax
from jax.experimental import pallas as pl
from jax.experimental.pallas import tpu as pltpu
from jax.sharding import PartitionSpec as P

EXPERTS = 64
WAVE = 1
MOST = 48
F32 = jnp.float32
BF16 = jnp.bfloat16


def dot(a, b, dims):
    return lax.dot_general(a, b, (dims, ((), ())), preferred_element_type=F32)


MESH = pl.DeviceIdType.MESH
HBM = pl.BlockSpec(memory_space=pltpu.MemorySpace.HBM)
VMEM = pl.BlockSpec(memory_space=pltpu.MemorySpace.VMEM)


class Place:
    def __init__(self, groups):
        self.groups = groups
        self.e = lax.axis_index("expert")
        f = lax.axis_index("fsdp")
        self.f = f
        self.chip = f // 2
        self.pair = f + 1 - 2 * (f % 2)
        bit_x, bit_y = self.chip % 2, self.chip // 2
        self.to_x, self.to_y = f + 2 - 4 * bit_x, f + 4 - 8 * bit_y
        self.chip_x, self.chip_y = self.chip + 1 - 2 * bit_x, self.chip + 2 - 4 * bit_y
        self.chip_far = 3 - self.chip

    def barrier(self, rows):
        sem = pltpu.get_barrier_semaphore()
        peers = [(self.e, self.to_x), (self.e, self.to_y)]
        if rows:
            for step in range(self.groups):
                there = (self.e + step) % self.groups
                peers.append((there, self.pair))
                if step:
                    peers.append((there, self.f))
        for peer in peers:
            pl.semaphore_signal(sem, inc=1, device_id=peer, device_id_type=MESH)
        pl.semaphore_wait(sem, len(peers))

    def rows(self, src, dst, which, send, recv, local):
        copies = []
        for half in range(2):
            for step in range(self.groups):
                there = (self.e + step) % self.groups
                if half == 0 and step == 0:
                    copy = pltpu.make_async_copy(
                        src.at[0, self.e], dst.at[0, self.e], local.at[which]
                    )
                else:
                    copy = pltpu.make_async_remote_copy(
                        src_ref=src.at[half, there],
                        dst_ref=dst.at[half, self.e],
                        send_sem=send.at[which, half, step],
                        recv_sem=recv.at[which, half, step],
                        device_id=(there, self.pair if half else self.f),
                        device_id_type=MESH,
                    )
                copy.start()
                copies.append(copy)
        return copies

    def send(self, src, dst, send, recv, index, to):
        copy = pltpu.make_async_remote_copy(
            src_ref=src,
            dst_ref=dst,
            send_sem=send.at[index],
            recv_sem=recv.at[index],
            device_id=(self.e, to),
            device_id_type=MESH,
        )
        copy.start()
        return copy


def gather_kernel(groups, count, n_rows, *refs):
    ws, picks = refs[:count], refs[count : count + n_rows]
    refs = refs[count + n_rows :]
    toks, refs = refs[:n_rows], refs[n_rows:]
    fulls, ins = refs[:count], refs[count : count + n_rows]
    xs, ws_send, ws_recv, ws_local, x_send, x_recv, x_local = refs[count + n_rows :]
    at = Place(groups)
    half = ws[0].shape[0] // 2
    at.barrier(n_rows > 0)
    pending, first = [], []
    for i in range(count):
        mine = fulls[i].at[at.chip]
        first.append(
            (
                at.send(ws[i], mine, ws_send, ws_recv, 4 * i, at.to_x),
                at.send(ws[i], mine, ws_send, ws_recv, 4 * i + 1, at.to_y),
            )
        )
        keep = pltpu.make_async_copy(ws[i], mine, ws_local.at[i])
        keep.start()
        pending.append(keep)
    block = ws[0].shape[0]
    for j in range(n_rows):
        for half_of in range(2):
            odd = at.f % 2 if half_of == 0 else 1 - at.f % 2
            for k in range(4):
                cols = pl.ds(pl.multiple_of((2 * k + odd) * block, block), block)
                part = dot(picks[j][...], toks[j][:, cols], ((0,), (0,))).astype(BF16)
                xs[j, half_of, :, :, pl.ds(k * block, block)] = part.reshape(
                    groups, MOST, block
                )
        pending += at.rows(xs.at[j], ins[j], j, x_send, x_recv, x_local)
    for i in range(count):
        by_x, by_y = first[i]
        by_x.wait_recv()
        part = fulls[i].at[at.chip_x, pl.ds(0, half)]
        pending.append(at.send(part, part, ws_send, ws_recv, 4 * i + 2, at.to_y))
        by_y.wait_recv()
        part = fulls[i].at[at.chip_y, pl.ds(half, half)]
        pending.append(at.send(part, part, ws_send, ws_recv, 4 * i + 3, at.to_x))
        by_x.wait_send()
        by_y.wait_send()
    for copy in pending:
        copy.wait()


def gather_call(groups, ws, picks, toks):
    count, n_rows = len(ws), len(toks)
    shape = (2, groups, MOST, toks[0].shape[1] // 2)
    dma = pltpu.SemaphoreType.DMA
    return pl.pallas_call(
        functools.partial(gather_kernel, groups, count, n_rows),
        out_shape=[jax.ShapeDtypeStruct((4,) + w.shape, BF16) for w in ws]
        + [jax.ShapeDtypeStruct(shape, BF16)] * n_rows,
        in_specs=[VMEM] * (count + 2 * n_rows),
        out_specs=[HBM] * (count + n_rows),
        scratch_shapes=[
            pltpu.VMEM((n_rows,) + shape, BF16),
            dma((4 * count,)),
            dma((4 * count,)),
            dma((count,)),
            dma((n_rows, 2, groups)),
            dma((n_rows, 2, groups)),
            dma((n_rows,)),
        ],
        compiler_params=pltpu.CompilerParams(
            collective_id=0, has_side_effects=True, vmem_limit_bytes=24 * 2**20
        ),
    )(*ws, *picks, *toks)


def scatter_kernel(groups, *refs):
    row_in, out_grad, hidden, gate_grad, up_grad, w_gate, w_up, w_down = refs[:8]
    owns, from_x, from_y, backs = refs[8:11], refs[11:14], refs[14:17], refs[17:19]
    term, xs, far_x, far_y, sum_x, sum_y, others = refs[19:26]
    t_send, t_recv, x_send, x_recv, x_local, a_send, a_recv = refs[26:]
    at = Place(groups)
    block = term.shape[2]
    half = block // 2
    top, low = pl.ds(0, half), pl.ds(half, half)
    at.barrier(True)
    pending, first = [], []
    factors = ((out_grad, hidden), (row_in, gate_grad), (row_in, up_grad))
    rows = hidden.shape[0]
    swaps = [
        at.send(act, others.at[i], a_send, a_recv, i, at.pair)
        for i, (_, act) in enumerate(factors)
    ]

    def product(i, chip):
        a, b = factors[i]
        cols = pl.ds(pl.multiple_of(chip * block, block), block)
        own = dot(a[pl.ds(0, rows), cols], b[...], ((0,), (0,)))
        return (own + dot(a[pl.ds(rows, rows), cols], others[i], ((0,), (0,)))).astype(BF16)

    def send(i, n, src, dst, to):
        return at.send(src, dst, t_send, t_recv, 6 * i + n, to)

    for i in range(3):
        swaps[i].wait()
        term[i, 0] = product(i, at.chip_far)
        first.append(
            (
                send(i, 0, term.at[i, 0, top], far_x.at[i], at.to_x),
                send(i, 1, term.at[i, 0, low], far_y.at[i], at.to_y),
            )
        )
        term[i, 1] = product(i, at.chip_x)
        pending.append(send(i, 2, term.at[i, 1, top], from_x[i].at[top], at.to_x))
        term[i, 2] = product(i, at.chip_y)
        pending.append(send(i, 3, term.at[i, 2, low], from_y[i].at[low], at.to_y))
    turned = ((1,), (1,))
    for slot in range(2):
        act = others[0] if slot else hidden[...]
        xs[0, slot] = dot(act, w_down[...], turned).astype(BF16).reshape(xs.shape[2:])
    pending += at.rows(xs.at[0], backs[0], 0, x_send, x_recv, x_local)
    for slot in range(2):
        g, u = (others[1], others[2]) if slot else (gate_grad[...], up_grad[...])
        back = dot(g, w_gate[...], turned) + dot(u, w_up[...], turned)
        xs[1, slot] = back.astype(BF16).reshape(xs.shape[2:])
    pending += at.rows(xs.at[1], backs[1], 1, x_send, x_recv, x_local)
    for i in range(3):
        by_x, by_y = first[i]
        by_x.wait_recv()
        sum_y[i] = (term[i, 2, top].astype(F32) + far_x[i].astype(F32)).astype(BF16)
        pending.append(send(i, 4, sum_y.at[i], from_y[i].at[top], at.to_y))
        by_y.wait_recv()
        sum_x[i] = (term[i, 1, low].astype(F32) + far_y[i].astype(F32)).astype(BF16)
        pending.append(send(i, 5, sum_x.at[i], from_x[i].at[low], at.to_x))
        owns[i][...] = product(i, at.chip)
        by_x.wait_send()
        by_y.wait_send()
    for copy in pending:
        copy.wait()


def scatter_call(groups, block, row_in, out_grad, acts, ws):
    dma = pltpu.SemaphoreType.DMA
    ff = acts[0].shape[1]
    shape = (2, groups, MOST, row_in.shape[1])
    piece = pltpu.VMEM((3, block // 2, ff), BF16)
    return pl.pallas_call(
        functools.partial(scatter_kernel, groups),
        out_shape=[jax.ShapeDtypeStruct((block, ff), BF16)] * 9
        + [jax.ShapeDtypeStruct(shape, BF16)] * 2,
        in_specs=[VMEM] * 8,
        out_specs=[VMEM] * 3 + [HBM] * 8,
        scratch_shapes=[
            pltpu.VMEM((3, 3, block, ff), BF16),
            pltpu.VMEM((2,) + shape, BF16),
            piece,
            piece,
            piece,
            piece,
            pltpu.VMEM((3,) + acts[0].shape, BF16),
            dma((18,)),
            dma((18,)),
            dma((2, 2, groups)),
            dma((2, 2, groups)),
            dma((2,)),
            dma((3,)),
            dma((3,)),
        ],
        compiler_params=pltpu.CompilerParams(
            collective_id=1, has_side_effects=True, vmem_limit_bytes=48 * 2**20
        ),
    )(row_in, out_grad, *acts, *ws)


def routes(expert_ids, gate_vals, groups):
    per_index = EXPERTS // groups
    window = WAVE * groups
    tok_count = expert_ids.shape[0]
    local_index = expert_ids % per_index
    window_slot = jnp.where(
        local_index < WAVE, expert_ids // per_index * WAVE + local_index, window
    )
    slot_is = window_slot[:, :, None] == jnp.arange(window, dtype=jnp.int32)[None, None, :]
    chosen = jnp.any(slot_is, axis=1)
    gate_of = jnp.sum(jnp.where(slot_is, gate_vals.astype(F32)[:, :, None], 0.0), axis=1)
    tok = jnp.arange(tok_count, dtype=jnp.int32)
    before = (tok[:, None] > tok[None, :]).astype(BF16)
    rank = dot(before, chosen.astype(BF16), ((1,), (0,))).astype(jnp.int32)
    place = chosen[:, :, None] & (
        rank[:, :, None] == jnp.arange(MOST, dtype=jnp.int32)[None, None, :]
    )
    pick = place.astype(BF16).reshape(tok_count, window * MOST)
    weighted = (
        jnp.where(place, gate_of[:, :, None], 0.0).astype(BF16).reshape(tok_count, window * MOST)
    )
    return slot_is, place, pick, weighted


def on_device(tokens, expert_ids, gate_vals, w_gate, w_up, w_down, cotangent):
    groups = lax.axis_size("expert")
    columns = lax.axis_size("fsdp")
    side = lax.axis_index("fsdp") % 2
    tok_count, width = tokens.shape
    block = w_gate.shape[1]
    rows = groups * MOST
    sides = [[i for i in range(columns) if i % 2 == s] for s in (0, 1)]
    pairs = [(i, i ^ 1) for i in range(columns)]

    def swap(x):
        return lax.ppermute(x, "fsdp", pairs)

    def gather(w):
        return lax.all_gather(w[0], "fsdp", axis_index_groups=sides, axis=0, tiled=True)

    def scatter(x):
        return lax.psum_scatter(
            x.astype(BF16), "fsdp", scatter_dimension=0, axis_index_groups=sides, tiled=True
        ).astype(F32)[None]

    def cut(x, odd):
        return jnp.concatenate(
            [x[:, (2 * k + odd) * block : (2 * k + odd + 1) * block] for k in range(columns // 2)],
            axis=1,
        )

    def halves(x):
        even, odd = cut(x, 0), cut(x, 1)
        return jnp.where(side == 0, even, odd), jnp.where(side == 0, odd, even)

    def whole_rows(mine, other):
        even, odd = jnp.where(side == 0, mine, other), jnp.where(side == 0, other, mine)
        parts = []
        for k in range(columns // 2):
            here = slice(k * block, (k + 1) * block)
            parts += [even[:, here], odd[:, here]]
        return jnp.concatenate(parts, axis=1)

    def exchange(mine, other):
        packed = jnp.stack(
            [mine.reshape(groups, MOST, width // 2), other.reshape(groups, MOST, width // 2)],
            axis=1,
        )
        there = lax.all_to_all(packed, "expert", split_axis=0, concat_axis=0, tiled=True)
        return there[:, 0].reshape(rows, width // 2), there[:, 1].reshape(rows, width // 2)

    square = columns == 8
    slot_is, place, pick, weighted = routes(expert_ids, gate_vals, groups)
    first = ((0,), (0,))
    if square:
        *full, row_in, out_grad = gather_call(
            groups, [w_gate[0], w_up[0], w_down[0]], [pick, weighted], [tokens, cotangent]
        )
        full_gate, full_up, full_down = (w.reshape(width // 2, w.shape[2]) for w in full)
        row_in = row_in.reshape(2 * rows, width // 2)
        out_grad = out_grad.reshape(2 * rows, width // 2)
    else:
        full_gate, full_up, full_down = gather(w_gate), gather(w_up), gather(w_down)
        row_mine, row_other = exchange(*halves(dot(pick, tokens, first).astype(BF16)))
        og_mine, og_other = exchange(*halves(dot(weighted, cotangent, first).astype(BF16)))
        row_in = jnp.concatenate([row_mine, swap(row_other)], axis=0)
        out_grad = jnp.concatenate([og_mine, swap(og_other)], axis=0)

    def summed(x):
        return x[:rows] + swap(x[rows:].astype(BF16)).astype(F32)

    def both(x):
        return jnp.concatenate([x, swap(x)], axis=0)

    plain, turned = ((1,), (0,)), ((1,), (1,))
    gate_pre = summed(dot(row_in, full_gate, plain))
    up_pre = summed(dot(row_in, full_up, plain))
    sigmoid_g = jax.nn.sigmoid(gate_pre)
    hidden = (gate_pre * sigmoid_g * up_pre).astype(BF16)
    hidden_grad = summed(dot(out_grad, full_down, plain))
    gate_grad = (
        hidden_grad * up_pre * sigmoid_g * (1.0 + gate_pre * (1.0 - sigmoid_g))
    ).astype(BF16)
    up_grad = (hidden_grad * gate_pre * sigmoid_g).astype(BF16)
    if square:
        got = scatter_call(
            groups,
            block,
            row_in,
            out_grad,
            [hidden, gate_grad, up_grad],
            [full_gate, full_up, full_down],
        )
        grad_w_down, grad_w_gate, grad_w_up = (
            (got[i].astype(F32) + got[3 + i].astype(F32) + got[6 + i].astype(F32))[None]
            for i in range(3)
        )
        outs, grads = ([r[i].reshape(rows, width // 2) for i in (0, 1)] for r in got[9:])
    else:
        hidden, gate_grad, up_grad = both(hidden), both(gate_grad), both(up_grad)
        grad_w_down = scatter(dot(out_grad, hidden, first))
        grad_w_gate = scatter(dot(row_in, gate_grad, first))
        grad_w_up = scatter(dot(row_in, up_grad, first))
        expert_out = dot(hidden, full_down, turned).astype(BF16)
        slot_grad = (
            dot(gate_grad, full_gate, turned) + dot(up_grad, full_up, turned)
        ).astype(BF16)
        outs = exchange(expert_out[:rows], swap(expert_out[rows:]))
        grads = exchange(slot_grad[:rows], swap(slot_grad[rows:]))

    slot_out = whole_rows(*outs)
    output = dot(weighted, slot_out, plain).astype(BF16)
    grad_tokens = dot(pick, whole_rows(*grads), plain).astype(BF16)
    met = dot(cotangent, slot_out, turned)
    met = jnp.sum(jnp.where(place, met.reshape(place.shape), 0.0), axis=2)
    grad_gates = jnp.sum(jnp.where(slot_is, met[:, None, :], 0.0), axis=2)
    return (output, grad_tokens, grad_gates, grad_w_gate, grad_w_up, grad_w_down)


def solution(mesh):
    token = P(("expert", "fsdp"), None)
    weight = P("expert", "fsdp", None)
    return jax.shard_map(
        on_device,
        mesh=mesh,
        in_specs=(token, token, token, weight, weight, weight, token),
        out_specs=(token, token, token, weight, weight, weight),
        check_vma=False,
    )
```

profile of v0, /device:TPU:0, one launch (start us, length us, event | category | flops | bytes accessed | tf_op | source)
XLA Modules:
  0.0 187.4 jit_solution(5396127582933932212)
XLA Ops:
  0.7 0.9 fusion.3
  2.1 0.7 convert_element_type.71
  3.1 1.1 copy-done.7
  4.2 1.1 copy-done.8
  5.4 1.1 copy-done.9
  6.5 77.6 %shard_map.118 = (bf16[4,256,1408]{2,1,0:T(8,128)(2,1)S(1)}, bf16[4,256,1408]{2,1,0:T(8,128)(2,1)S(1)}, bf16[4,256,1408]{2,1,0:T(8,128)(2,1)S(1)}, bf16[2,4,48,1...) custom-call(bf16[256,1408]{1,0:T(8,128)(2,1)S(1)} %bitcast.48, bf16[256,1408]{1,0:T(8,128)(2,1)S(1)} %bitcast.49, ...), custom_call_target="tpu_custom_call" | custom-call | tf_op jit(solution)/shard_map/pallas_call | solution.py:137
  84.2 1.4 fusion.8
  85.7 1.5 slice.174
  87.2 1.4 fusion.7
  88.6 0.9 slice.175
  89.6 0.5 collective-permute-start
  90.1 1.4 fusion.9
  91.5 1.0 slice.173
  92.4 0.6 copy-done.13
  93.1 2.3 %collective-permute-done.2 = bf16[192,1408]{1,0:T(8,128)(2,1)} collective-permute-done((bf16[192,1408]{1,0:T(8,128)(2,1)}, bf16[192,1408]{1,0:T(8,128)(2,1)}, u32[]{:S(2)}, u32[]{:S(2)}) %collective-permute-start.2) | collective-permute-done | bytes 540704 | tf_op jit(solution)/shard_map/ppermute | solution.py:291
  95.4 2.8 %multiply_convert_fusion = (bf16[192,1408]{1,0:T(8,128)(2,1)S(1)}, bf16[192,1408]{1,0:T(8,128)(2,1)S(1)}, bf16[192,1408]{1,0:T(8,128)(2,1)S(1)}) fusion(bf16[192,1408]{1,0:T(8,128)(2,1)} %collective-permute-done.2, f32[384,1408]{1,0:T(8,128)} %copy-done.13, bf16[192,1408]{1,0:T(8,128)(2,1)} %collective-permute-done, f32[384,1408]{1,0:T(8,128)} %copy-done.12, ...), kind=kLoop, calls=%fused_computation.12 | loop fusion | flops 5947392 | bytes 6488064 | tf_op jit(solution)/shard_map/convert_element_type | solution.py:359
  98.1 79.8 %shard_map.119 = (bf16[256,1408]{1,0:T(8,128)(2,1)S(1)}, bf16[256,1408]{1,0:T(8,128)(2,1)S(1)}, bf16[256,1408]{1,0:T(8,128)(2,1)S(1)}, bf16[256,1408]{1,0:T(8,12...) custom-call(bf16[384,1024]{1,0:T(8,128)(2,1)} %bitcast.45, ...), custom_call_target="tpu_custom_call" | custom-call | tf_op jit(solution)/shard_map/pallas_call | solution.py:228
  177.9 1.5 broadcast_select_fusion
  179.6 1.4 convolution_convert_fusion.1
  181.0 0.5 fusion.10
  181.7 1.4 convolution_convert_fusion
  183.1 0.6 select_reduce_fusion.1
  183.8 1.4 add_bitcast_fusion.2
  185.3 2.0 %add_bitcast_fusion = (f32[1,256,1408]{2,1,0:T(8,128)}, f32[1,256,1408]{2,1,0:T(8,128)}) fusion(bf16[256,1408]{1,0:T(8,128)(2,1)S(1)} %copy-done.14, bf16[256,1408]{1,0:T(8,128)(2,1)S(1)} %get-tuple-element.36, bf16[256,1408]{1,0:T(8,128)(2,1)S(1)} %get-tuple-element.35, bf16[256,1408]{1,0:T(8,128)(2,1)S(1)} %copy-done.15, ...), kind=kLoop, calls=%fused_computation.2 | loop fusion | flops 3604480 | bytes 7208960 | tf_op jit(solution)/shard_map/broadcast_in_dim | solution.py:370
  (64 shorter events, 1.5 us)
Async XLA Ops:
  0.6 2.5 %copy-start = (bf16[256,2048]{1,0:T(8,128)(2,1)S(1)}, bf16[256,2048]{1,0:T(8,128)(2,1)}, u32[]{:S(2)}) copy-start(bf16[256,2048]{1,0:T(8,128)(2,1)} %refs_6_.1) | copy-start | bytes 3145732
  0.6 2.5 %copy-start.4 = (bf16[256,2048]{1,0:T(8,128)(2,1)S(1)}, bf16[256,2048]{1,0:T(8,128)(2,1)}, u32[]{:S(2)}) copy-start(bf16[256,2048]{1,0:T(8,128)(2,1)} %refs_5_.1) | copy-start | bytes 3145732
  3.1 1.1 copy-start.7
  4.2 1.1 copy-start.8
  5.4 1.1 copy-start.9
  84.1 1.6 copy-start.2
  84.1 3.1 %copy-start.1 = (bf16[4,256,1408]{2,1,0:T(8,128)(2,1)}, bf16[4,256,1408]{2,1,0:T(8,128)(2,1)S(1)}, u32[]{:S(2)}) copy-start(bf16[4,256,1408]{2,1,0:T(8,128)(2,1)S(1)} %get-tuple-element.24) | copy-start | bytes 8650756
  84.1 4.5 %copy-start.5 = (bf16[2,4,48,1024]{3,2,1,0:T(8,128)(2,1)}, bf16[2,4,48,1024]{3,2,1,0:T(8,128)(2,1)S(1)}, u32[]{:S(2)}) copy-start(bf16[2,4,48,1024]{3,2,1,0:T(8,128)(2,1)S(1)} %get-tuple-element.22) | copy-start | bytes 2359300
  84.1 5.9 %copy-start.3 = (bf16[4,256,1408]{2,1,0:T(8,128)(2,1)}, bf16[4,256,1408]{2,1,0:T(8,128)(2,1)S(1)}, u32[]{:S(2)}) copy-start(bf16[4,256,1408]{2,1,0:T(8,128)(2,1)S(1)} %get-tuple-element.26) | copy-start | bytes 8650756
  84.1 5.9 %copy-start.6 = (bf16[2,4,48,1024]{3,2,1,0:T(8,128)(2,1)}, bf16[2,4,48,1024]{3,2,1,0:T(8,128)(2,1)S(1)}, u32[]{:S(2)}) copy-start(bf16[2,4,48,1024]{3,2,1,0:T(8,128)(2,1)S(1)} %get-tuple-element.23) | copy-start | bytes 2359300
  85.7 2.9 %copy-start.10 = (f32[384,1408]{1,0:T(8,128)}, f32[384,1408]{1,0:T(8,128)S(1)}, u32[]{:S(2)}) copy-start(f32[384,1408]{1,0:T(8,128)S(1)} %fusion.8) | copy-start | bytes 6488068
  87.2 5.9 %collective-permute-start.1 = (bf16[192,1408]{1,0:T(8,128)(2,1)}, bf16[192,1408]{1,0:T(8,128)(2,1)}, u32[]{:S(2)}, u32[]{:S(2)}) collective-permute-start(bf16[192,1408]{1,0:T(8,128)(2,1)} %slice.174), channel_id=1, source_target_pairs={{0,1},{1,0},{2,3},{3,2},{4,5},{5,4},{6,7},{7,6},{8,9},{9,8},{10,11... | collective-permute-start | bytes 1622024 | tf_op jit(solution)/shard_map/ppermute | solution.py:291
  88.6 2.9 %copy-start.12 = (f32[384,1408]{1,0:T(8,128)}, f32[384,1408]{1,0:T(8,128)S(1)}, u32[]{:S(2)}) copy-start(f32[384,1408]{1,0:T(8,128)S(1)} %fusion.7) | copy-start | bytes 6488068
  89.6 3.5 %collective-permute-start = (bf16[192,1408]{1,0:T(8,128)(2,1)}, bf16[192,1408]{1,0:T(8,128)(2,1)}, u32[]{:S(2)}, u32[]{:S(2)}) collective-permute-start(bf16[192,1408]{1,0:T(8,128)(2,1)} %slice.175), channel_id=1, source_target_pairs={{0,1},{1,0},{2,3},{3,2},{4,5},{5,4},{6,7},{7,6},{8,9},{9,8},{10,11... | collective-permute-start | bytes 1622024 | tf_op jit(solution)/shard_map/ppermute | solution.py:291
  90.1 5.3 %copy-start.11 = (f32[384,1408]{1,0:T(8,128)S(1)}, f32[384,1408]{1,0:T(8,128)}, u32[]{:S(2)}) copy-start(f32[384,1408]{1,0:T(8,128)} %copy-done.10) | copy-start | bytes 6488068
  91.5 1.6 copy-start.13
  93.1 2.3 %collective-permute-start.2 = (bf16[192,1408]{1,0:T(8,128)(2,1)}, bf16[192,1408]{1,0:T(8,128)(2,1)}, u32[]{:S(2)}, u32[]{:S(2)}) collective-permute-start(bf16[192,1408]{1,0:T(8,128)(2,1)} %slice.173), channel_id=1, source_target_pairs={{0,1},{1,0},{2,3},{3,2},{4,5},{5,4},{6,7},{7,6},{8,9},{9,8},{10,11... | collective-permute-start | bytes 1622024 | tf_op jit(solution)/shard_map/ppermute | solution.py:291
  181.6 2.2 %copy-start.16 = (bf16[256,1408]{1,0:T(8,128)(2,1)S(1)}, bf16[256,1408]{1,0:T(8,128)(2,1)}, u32[]{:S(2)}) copy-start(bf16[256,1408]{1,0:T(8,128)(2,1)} %get-tuple-element.31) | copy-start | bytes 2162692
  183.8 1.4 copy-start.14
  183.8 1.6 copy-start.15
where the time goes:
time: 188 us; the launch traced here: 187 us
  Pallas kernels  157 us (84%)
  other arithmetic  10.1 us (5%)
  local copies, waits for them, and re-layouts  8.49 us (5%)
  matrix products  7.6 us (4%)
  waiting for transfers between devices  2.26 us (1%)
    pallas_call x1, Pallas kernels, scatter_call(): pl.pallas_call(functools.partial(scatter_kernel, groups), out_shape=[jax....  79.8 us
    pallas_call x1, Pallas kernels, gather_call(): pl.pallas_call(functools.partial(gather_kernel, groups, count, n_rows), o...  77.6 us
    dot_general x7, matrix products, dot(): return lax.dot_general(a, b, (dims, ((), ())), preferred_element_type=F32)  7.6 us
    unnamed x48, local copies, waits for them, and re-layouts  4.54 us
  transfers between devices with their start and end apart: 3, of which 1 were waited for; matrix products, arithmetic and copies ran while one was open for 2% of the time, Pallas kernels for 0%

commit v1 on v0

v1 whole, which is shorter than its diff:
```python
import functools

import jax
import jax.numpy as jnp
from jax import lax
from jax.experimental import pallas as pl
from jax.experimental.pallas import tpu as pltpu
from jax.sharding import PartitionSpec as P

EXPERTS = 64
WAVE = 1
MOST = 48
F32 = jnp.float32
BF16 = jnp.bfloat16


def dot(a, b, dims):
    return lax.dot_general(a, b, (dims, ((), ())), preferred_element_type=F32)


MESH = pl.DeviceIdType.MESH
HBM = pl.BlockSpec(memory_space=pltpu.MemorySpace.HBM)
VMEM = pl.BlockSpec(memory_space=pltpu.MemorySpace.VMEM)


class Place:
    def __init__(self, groups):
        self.groups = groups
        self.e = lax.axis_index("expert")
        f = lax.axis_index("fsdp")
        self.f = f
        self.core = f % 2
        self.x, self.y = (f // 2) % 2, f // 4
        self.pair = f + 1 - 2 * self.core
        self.to_x, self.to_y = f + 2 - 4 * self.x, f + 4 - 8 * self.y

    def barrier(self):
        sem = pltpu.get_barrier_semaphore()
        peers = [(self.e, self.pair)]
        for step in range(self.groups):
            there = (self.e + step) % self.groups
            peers += [(there, self.to_x), (there, self.to_y)]
            if step:
                peers.append((there, self.f))
        for peer in peers:
            pl.semaphore_signal(sem, inc=1, device_id=peer, device_id_type=MESH)
        pl.semaphore_wait(sem, len(peers))


class Copies:
    def __init__(self, send, recv, local):
        self.sems = send, recv, local
        self.remote = self.near = 0
        self.pending = []

    def send(self, src, dst, to):
        send, recv, _ = self.sems
        copy = pltpu.make_async_remote_copy(
            src_ref=src,
            dst_ref=dst,
            send_sem=send.at[self.remote],
            recv_sem=recv.at[self.remote],
            device_id=to,
            device_id_type=MESH,
        )
        self.remote += 1
        copy.start()
        self.pending.append(copy)
        return copy

    def keep(self, src, dst):
        copy = pltpu.make_async_copy(src, dst, self.sems[2].at[self.near])
        self.near += 1
        copy.start()
        return copy


GATE, UP, DOWN = range(3)
REMOTE = 80
LOCAL = 16


def layer_kernel(groups, *refs):
    ws, (pick, weighted, tokens, cotangent) = refs[:3], refs[3:7]
    owns, output, grad_tokens, met = refs[7:10], refs[10], refs[11], refs[12]
    full, xs, rows_in, acc, pre_out, pre_in, act = refs[13:20]
    pair_out, pair_in, sum_out, near_in, back_out, back_in, far_acc = refs[20:27]
    at, go = Place(groups), Copies(*refs[27:30])
    block, ff = ws[0].shape
    rows = groups * MOST
    half_d = 4 * block
    piece = block // 2
    mine, pair = (at.e, at.f), (at.e, at.pair)
    across = [(at.e, at.to_y), (at.e, at.to_y), (at.e, at.to_x)]
    beside = [(at.e, at.to_x), (at.e, at.to_x), (at.e, at.to_y)]
    spot = [at.y, at.y, at.x]

    def span(q, s):
        return pl.ds(pl.multiple_of((2 * q + s) * block, block), block)

    def chip_span(q):
        return pl.ds(pl.multiple_of(2 * q * block, 2 * block), 2 * block)

    def part(start, size):
        return pl.ds(pl.multiple_of(start, piece), size)

    at.barrier()

    def fetch(m):
        copies = []
        for p in range(2):
            where = part((2 * spot[m] + at.core) * block + p * piece, piece)
            copies.append(
                go.send(ws[m].at[pl.ds(p * piece, piece)], full.at[m, where], across[m])
            )
        return copies

    def near(m):
        where = span(spot[m], at.core)
        return go.send(ws[m], full.at[m, where], pair), go.keep(ws[m], full.at[m, where])

    def forward(m, copies):
        out = []
        for p, copy in enumerate(copies):
            copy.wait_recv()
            where = full.at[m, part((2 * (1 - spot[m]) + at.core) * block + p * piece, piece)]
            out.append(go.send(where, where, pair))
        return out

    def spread(src, dst, other, half):
        copies = []
        for step in range(groups):
            there = (at.e + step) % groups
            if half == 0 and step == 0:
                copies.append(go.keep(src.at[0, at.e], dst.at[0, at.e]))
            else:
                copies.append(
                    go.send(src.at[half, there], dst.at[half, at.e], (there, other if half else at.f))
                )
        return copies

    def wait_in(copies):
        for copy in copies:
            if copy.is_remote:
                copy.wait_recv()
            else:
                copy.wait()

    def x_cols(half, k):
        x = 1 - at.x if half else at.x
        return pl.ds(pl.multiple_of((4 * k + 2 * x) * block, 2 * block), 2 * block)

    def y_cols(half):
        y = 1 - at.y if half else at.y
        return pl.ds(pl.multiple_of(4 * y * block, half_d), half_d)

    shape = (groups, MOST, -1)
    down_first = ((0,), (0,))
    plain, turned = ((1,), (0,)), ((1,), (1,))

    from_gate = fetch(GATE)
    near_gate = near(GATE)
    x_rows = []
    for half in (1, 0):
        for k in range(2):
            val = dot(pick[...], tokens[:, x_cols(half, k)], down_first).astype(BF16)
            xs[0, half, :, :, pl.ds(2 * k * block, 2 * block)] = val.reshape(shape[:2] + (2 * block,))
        x_rows += spread(xs.at[0], rows_in.at[0], at.to_x, half)
    from_up = fetch(UP)
    from_down = fetch(DOWN)
    near_up, near_down = near(UP), near(DOWN)
    og_rows = []
    for half in (1, 0):
        val = dot(weighted[...], cotangent[:, y_cols(half)], down_first).astype(BF16)
        xs[1, half] = val.reshape(shape[:2] + (half_d,))
        og_rows += spread(xs.at[1], rows_in.at[1], at.to_y, half)

    def lhs(t, cols):
        return rows_in[t, :, :, :, cols].reshape(2 * rows, -1)

    def begin(m, t):
        acc[m] = dot(lhs(t, chip_span(spot[m])), full[m, chip_span(spot[m])], plain)

    def finish(m, t):
        other = 1 - spot[m]
        acc[m] += dot(lhs(t, chip_span(other)), full[m, chip_span(other)], plain)
        pre_out[m] = acc[m, pl.ds(rows, rows)].astype(BF16)
        return go.send(pre_out.at[m], pre_in.at[m], beside[m])

    def wait_near(copies):
        copies[0].wait_recv()
        copies[1].wait()

    far_gate = forward(GATE, from_gate)
    wait_in(x_rows)
    wait_near(near_gate)
    begin(GATE, 0)
    wait_in(far_gate)
    pre_gate = finish(GATE, 0)
    wait_near(near_up)
    begin(UP, 0)
    far_down = forward(DOWN, from_down)
    far_up = forward(UP, from_up)
    wait_in(far_up)
    pre_up = finish(UP, 0)
    wait_near(near_down)
    wait_in(far_down)
    wait_in(og_rows)
    begin(DOWN, 1)
    pre_down = finish(DOWN, 1)

    tile = 16

    def hidden_rows(i, _):
        r = pl.ds(pl.multiple_of(i * tile, tile), tile)
        g = acc[GATE, r] + pre_in[GATE, r].astype(F32)
        u = acc[UP, r] + pre_in[UP, r].astype(F32)
        acc[GATE, r] = g
        acc[UP, r] = u
        act[DOWN, r] = (g * jax.nn.sigmoid(g) * u).astype(BF16)
        return 0

    def grad_rows(i, _):
        r = pl.ds(pl.multiple_of(i * tile, tile), tile)
        g, u = acc[GATE, r], acc[UP, r]
        h = acc[DOWN, r] + pre_in[DOWN, r].astype(F32)
        s = jax.nn.sigmoid(g)
        act[GATE, r] = (h * u * s * (1.0 + g * (1.0 - s))).astype(BF16)
        act[UP, r] = (h * g * s).astype(BF16)
        return 0

    top, low = pl.ds(0, rows), pl.ds(rows, rows)

    def share(m):
        return go.send(act.at[m, top], act.at[m, low], beside[m])

    pre_gate.wait_recv()
    pre_up.wait_recv()
    lax.fori_loop(0, rows // tile, hidden_rows, 0)
    got_hidden = share(DOWN)
    pre_down.wait_recv()
    lax.fori_loop(0, rows // tile, grad_rows, 0)
    got_gate = share(GATE)
    got_up = share(UP)

    def term(m, t, q, s):
        return dot(lhs(t, span(q, s)), act[m], down_first)

    def grads(m, t):
        q, other = spot[m], 1 - spot[m]
        pair_out[m, 0] = term(m, t, other, 1 - at.core).astype(BF16)
        to_far = go.send(pair_out.at[m, 0], pair_in.at[m, 0], pair)
        far_acc[...] = term(m, t, other, at.core)
        to_far.wait_recv()
        sum_out[m] = (far_acc[...] + pair_in[m, 0].astype(F32)).astype(BF16)
        to_other = go.send(sum_out.at[m], near_in.at[m], across[m])
        pair_out[m, 1] = term(m, t, q, 1 - at.core).astype(BF16)
        to_pair = go.send(pair_out.at[m, 1], pair_in.at[m, 1], pair)
        owns[m][...] = term(m, t, q, at.core)
        return to_other, to_pair

    got_hidden.wait_recv()
    back = []
    for half in (1, 0):
        hid = act[DOWN, low] if half else act[DOWN, top]
        back_out[0, half] = dot(hid, full[DOWN], turned).astype(BF16).reshape(shape[:2] + (half_d,))
        back += spread(back_out.at[0], back_in.at[0], at.to_y, half)
    got_gate.wait_recv()
    ends = [None] * 3
    ends[GATE] = grads(GATE, 0)
    got_up.wait_recv()
    back_grad = []
    for half in (1, 0):
        r = low if half else top
        val = dot(act[GATE, r], full[GATE], turned) + dot(act[UP, r], full[UP], turned)
        back_out[1, half] = val.astype(BF16).reshape(shape[:2] + (half_d,))
        back_grad += spread(back_out.at[1], back_in.at[1], at.to_x, half)
    ends[UP] = grads(UP, 0)
    ends[DOWN] = grads(DOWN, 1)

    wait_in(back)
    total = None
    for half in range(2):
        slot = back_in[0, half].reshape(rows, half_d)
        output[:, y_cols(half)] = dot(weighted[...], slot, plain).astype(BF16)
        val = dot(cotangent[:, y_cols(half)], slot, turned)
        total = val if total is None else total + val
    met[...] = total
    wait_in(back_grad)
    for half in range(2):
        for k in range(2):
            slot = back_in[1, half, :, :, pl.ds(2 * k * block, 2 * block)].reshape(rows, 2 * block)
            grad_tokens[:, x_cols(half, k)] = dot(pick[...], slot, plain).astype(BF16)
    for m in (GATE, DOWN, UP):
        to_other, to_pair = ends[m]
        to_pair.wait_recv()
        to_other.wait_recv()
        owns[m][...] += pair_in[m, 1].astype(F32) + near_in[m].astype(F32)
    for copy in go.pending:
        copy.wait_send()


def layer_call(groups, ws, pick, weighted, tokens, cotangent):
    dma = pltpu.SemaphoreType.DMA
    block, ff = ws[0].shape
    tok, width = tokens.shape
    rows = groups * MOST
    wide = (2, 2, groups, MOST, width // 2)
    vmem = pltpu.VMEM
    return pl.pallas_call(
        functools.partial(layer_kernel, groups),
        out_shape=[jax.ShapeDtypeStruct((block, ff), F32)] * 3
        + [jax.ShapeDtypeStruct((tok, width), BF16)] * 2
        + [jax.ShapeDtypeStruct((tok, rows), F32)],
        in_specs=[HBM] * 3 + [VMEM] * 4,
        out_specs=[VMEM] * 6,
        scratch_shapes=[
            vmem((3, 4 * block, ff), BF16),
            vmem(wide, BF16),
            vmem(wide, BF16),
            vmem((3, 2 * rows, ff), F32),
            vmem((3, rows, ff), BF16),
            vmem((3, rows, ff), BF16),
            vmem((3, 2 * rows, ff), BF16),
            vmem((3, 2, block, ff), BF16),
            vmem((3, 2, block, ff), BF16),
            vmem((3, block, ff), BF16),
            vmem((3, block, ff), BF16),
            vmem(wide, BF16),
            vmem(wide, BF16),
            vmem((block, ff), F32),
            dma((REMOTE,)),
            dma((REMOTE,)),
            dma((LOCAL,)),
        ],
        compiler_params=pltpu.CompilerParams(
            collective_id=0, has_side_effects=True, vmem_limit_bytes=62 * 2**20
        ),
    )(*ws, pick, weighted, tokens, cotangent)


def routes(expert_ids, gate_vals, groups):
    per_index = EXPERTS // groups
    window = WAVE * groups
    tok_count = expert_ids.shape[0]
    local_index = expert_ids % per_index
    window_slot = jnp.where(
        local_index < WAVE, expert_ids // per_index * WAVE + local_index, window
    )
    slot_is = window_slot[:, :, None] == jnp.arange(window, dtype=jnp.int32)[None, None, :]
    chosen = jnp.any(slot_is, axis=1)
    gate_of = jnp.sum(jnp.where(slot_is, gate_vals.astype(F32)[:, :, None], 0.0), axis=1)
    tok = jnp.arange(tok_count, dtype=jnp.int32)
    before = (tok[:, None] > tok[None, :]).astype(BF16)
    rank = dot(before, chosen.astype(BF16), ((1,), (0,))).astype(jnp.int32)
    place = chosen[:, :, None] & (
        rank[:, :, None] == jnp.arange(MOST, dtype=jnp.int32)[None, None, :]
    )
    pick = place.astype(BF16).reshape(tok_count, window * MOST)
    weighted = (
        jnp.where(place, gate_of[:, :, None], 0.0).astype(BF16).reshape(tok_count, window * MOST)
    )
    return slot_is, place, pick, weighted


def on_device(tokens, expert_ids, gate_vals, w_gate, w_up, w_down, cotangent):
    groups = lax.axis_size("expert")
    columns = lax.axis_size("fsdp")
    side = lax.axis_index("fsdp") % 2
    tok_count, width = tokens.shape
    block = w_gate.shape[1]
    rows = groups * MOST
    sides = [[i for i in range(columns) if i % 2 == s] for s in (0, 1)]
    pairs = [(i, i ^ 1) for i in range(columns)]

    def swap(x):
        return lax.ppermute(x, "fsdp", pairs)

    def gather(w):
        return lax.all_gather(w[0], "fsdp", axis_index_groups=sides, axis=0, tiled=True)

    def scatter(x):
        return lax.psum_scatter(
            x.astype(BF16), "fsdp", scatter_dimension=0, axis_index_groups=sides, tiled=True
        ).astype(F32)[None]

    def cut(x, odd):
        return jnp.concatenate(
            [x[:, (2 * k + odd) * block : (2 * k + odd + 1) * block] for k in range(columns // 2)],
            axis=1,
        )

    def halves(x):
        even, odd = cut(x, 0), cut(x, 1)
        return jnp.where(side == 0, even, odd), jnp.where(side == 0, odd, even)

    def whole_rows(mine, other):
        even, odd = jnp.where(side == 0, mine, other), jnp.where(side == 0, other, mine)
        parts = []
        for k in range(columns // 2):
            here = slice(k * block, (k + 1) * block)
            parts += [even[:, here], odd[:, here]]
        return jnp.concatenate(parts, axis=1)

    def exchange(mine, other):
        packed = jnp.stack(
            [mine.reshape(groups, MOST, width // 2), other.reshape(groups, MOST, width // 2)],
            axis=1,
        )
        there = lax.all_to_all(packed, "expert", split_axis=0, concat_axis=0, tiled=True)
        return there[:, 0].reshape(rows, width // 2), there[:, 1].reshape(rows, width // 2)

    square = columns == 8
    slot_is, place, pick, weighted = routes(expert_ids, gate_vals, groups)
    first = ((0,), (0,))
    if square:
        *grad_w, output, grad_tokens, met = layer_call(
            groups, [w_gate[0], w_up[0], w_down[0]], pick, weighted, tokens, cotangent
        )
        met = jnp.sum(jnp.where(place, met.reshape(place.shape), 0.0), axis=2)
        grad_gates = jnp.sum(jnp.where(slot_is, met[:, None, :], 0.0), axis=2)
        return (output, grad_tokens, grad_gates, *(g[None] for g in grad_w))
    full_gate, full_up, full_down = gather(w_gate), gather(w_up), gather(w_down)
    row_mine, row_other = exchange(*halves(dot(pick, tokens, first).astype(BF16)))
    og_mine, og_other = exchange(*halves(dot(weighted, cotangent, first).astype(BF16)))
    row_in = jnp.concatenate([row_mine, swap(row_other)], axis=0)
    out_grad = jnp.concatenate([og_mine, swap(og_other)], axis=0)

    def summed(x):
        return x[:rows] + swap(x[rows:].astype(BF16)).astype(F32)

    def both(x):
        return jnp.concatenate([x, swap(x)], axis=0)

    plain, turned = ((1,), (0,)), ((1,), (1,))
    gate_pre = summed(dot(row_in, full_gate, plain))
    up_pre = summed(dot(row_in, full_up, plain))
    sigmoid_g = jax.nn.sigmoid(gate_pre)
    hidden = (gate_pre * sigmoid_g * up_pre).astype(BF16)
    hidden_grad = summed(dot(out_grad, full_down, plain))
    gate_grad = (
        hidden_grad * up_pre * sigmoid_g * (1.0 + gate_pre * (1.0 - sigmoid_g))
    ).astype(BF16)
    up_grad = (hidden_grad * gate_pre * sigmoid_g).astype(BF16)
    hidden, gate_grad, up_grad = both(hidden), both(gate_grad), both(up_grad)
    grad_w_down = scatter(dot(out_grad, hidden, first))
    grad_w_gate = scatter(dot(row_in, gate_grad, first))
    grad_w_up = scatter(dot(row_in, up_grad, first))
    expert_out = dot(hidden, full_down, turned).astype(BF16)
    slot_grad = (dot(gate_grad, full_gate, turned) + dot(up_grad, full_up, turned)).astype(BF16)
    outs = exchange(expert_out[:rows], swap(expert_out[rows:]))
    grads = exchange(slot_grad[:rows], swap(slot_grad[rows:]))

    slot_out = whole_rows(*outs)
    output = dot(weighted, slot_out, plain).astype(BF16)
    grad_tokens = dot(pick, whole_rows(*grads), plain).astype(BF16)
    met = dot(cotangent, slot_out, turned)
    met = jnp.sum(jnp.where(place, met.reshape(place.shape), 0.0), axis=2)
    grad_gates = jnp.sum(jnp.where(slot_is, met[:, None, :], 0.0), axis=2)
    return (output, grad_tokens, grad_gates, grad_w_gate, grad_w_up, grad_w_down)


def solution(mesh):
    token = P(("expert", "fsdp"), None)
    weight = P("expert", "fsdp", None)
    return jax.shard_map(
        on_device,
        mesh=mesh,
        in_specs=(token, token, token, weight, weight, weight, token),
        out_specs=(token, token, token, weight, weight, weight),
        check_vma=False,
    )
```

time: 188 us -> 140 us (0.74)
  Pallas kernels: 157 us -> 125 us
  matrix products: 7.6 us -> 0.16 us
  other arithmetic: 10.1 us -> 3.56 us
  waiting for transfers between devices: 2.26 us -> 0 us
  local copies, waits for them, and re-layouts: 8.49 us -> 10.6 us
    pallas_call x2 -> x1, Pallas kernels: 157 us -> 125 us  [layer_call(): pl.pallas_call(functools.partial(layer_kernel, groups), out_shape=[jax.Sh...]
    dot_general x7 -> x1, matrix products: 7.6 us -> 0.16 us  [dot(): return lax.dot_general(a, b, (dims, ((), ())), preferred_element_type=F32)]
    unnamed x48 -> x13, local copies, waits for them, and re-layouts: 4.54 us -> 8.91 us
    broadcast_in_dim x2 -> x0, other arithmetic: 3.46 us -> none  [on_device(): (got[i].astype(F32) + got[3 + i].astype(F32) + got[6 + i].astype(F32))[None]]
    slice x3 -> x0, local copies, waits for them, and re-layouts: 3.39 us -> none  [summed(): return x[:rows] + swap(x[rows:].astype(BF16)).astype(F32)]
    convert_element_type x1 -> x0, other arithmetic: 2.78 us -> none  [on_device(): up_grad = (hidden_grad * gate_pre * sigmoid_g).astype(BF16)]
    ppermute x3 -> x0, waiting for transfers between devices: 2.26 us -> none  [swap(): return lax.ppermute(x, 'fsdp', pairs)]
  transfers between devices with their start and end apart: 3 -> 0, of which waited for: 1 -> 0; matrix products, arithmetic and copies ran while one was open for 2% -> 0% of each run, Pallas kernels for 0% -> 0%
where the time goes in v1:
time: 140 us
  Pallas kernels  125 us (89%)
  local copies, waits for them, and re-layouts  10.6 us (8%)
  other arithmetic  3.56 us (3%)
    pallas_call x1, Pallas kernels, layer_call(): pl.pallas_call(functools.partial(layer_kernel, groups), out_shape=[jax.Sh...  125 us
    unnamed x13, local copies, waits for them, and re-layouts  8.91 us

profile of v1, /device:TPU:0, one launch (start us, length us, event | category | flops | bytes accessed | tf_op | source)
XLA Modules:
  0.0 139.9 jit_solution(1027928742232257510)
XLA Ops:
  0.6 0.1 eq.46
  0.7 0.7 fusion.3
  1.5 0.2 convolution_convert_fusion
  1.6 0.7 convert_element_type.18
  2.4 0.2 copy.30
  2.6 0.1 copy.31
  2.7 0.1 copy.29
  2.8 0.7 select_convert_fusion
  3.6 0.7 convert_element_type.17.refs_3_
  4.2 124.9 %shard_map.118 = (f32[256,1408]{1,0:T(8,128)}, f32[256,1408]{1,0:T(8,128)}, f32[256,1408]{1,0:T(8,128)}, bf16[256,2048]{1,0:T(8,128)(2,1)}, bf16[256,2048]{1,0:T(8,128)(2,1)}, /*index=5*/f32[256,192]{1,0:T(8,128)}) custom-call(bf16[256,1408]{1,0:T(8,128)(2,1)} %bitcast.16, bf16[256,1408]{1,0:T(8,128)(2,1)} %bitcast.17, bf16[256,1408]{1,0:T(8,128)(2,1)} %bitcast.18, ...), custom_call_target="tpu_custom_call" | custom-call | tf_op jit(solution)/shard_map/pallas_call | solution.py:310
  129.1 0.0 copy-start.3
  129.2 1.1 copy.32
  130.3 0.1 select_reduce_fusion
  130.4 0.6 select_reduce_fusion.1
  131.0 2.3 %copy.38 = bf16[256,2048]{1,0:T(8,128)(2,1)} copy(bf16[256,2048]{1,0:T(8,128)(2,1)} %get-tuple-element.26) | data formatting | bytes 2097152
  133.3 0.0 copy-done.3
  133.3 0.0 copy-start.2
  133.3 1.0 copy.39
  134.3 0.8 copy-done.2
  135.0 1.1 copy.40
  136.1 0.8 copy-done.1
  136.9 1.1 copy.41
  138.0 0.8 copy-done
  138.8 1.1 copy.42
  (8 shorter events, 0.1 us)
Async XLA Ops:
  129.1 4.2 %copy-start.3 = (bf16[256,2048]{1,0:T(8,128)(2,1)S(1)}, bf16[256,2048]{1,0:T(8,128)(2,1)}, u32[]{:S(2)}) copy-start(bf16[256,2048]{1,0:T(8,128)(2,1)} %get-tuple-element.27) | copy-start | bytes 3145732
  133.3 1.7 %copy-start.2 = (f32[256,1408]{1,0:T(8,128)S(1)}, f32[256,1408]{1,0:T(8,128)}, u32[]{:S(2)}) copy-start(f32[256,1408]{1,0:T(8,128)} %get-tuple-element.15) | copy-start | bytes 4325380
  135.0 1.9 %copy-start.1 = (f32[256,1408]{1,0:T(8,128)S(1)}, f32[256,1408]{1,0:T(8,128)}, u32[]{:S(2)}) copy-start(f32[256,1408]{1,0:T(8,128)} %get-tuple-element.16) | copy-start | bytes 4325380
  136.9 1.9 %copy-start = (f32[256,1408]{1,0:T(8,128)S(1)}, f32[256,1408]{1,0:T(8,128)}, u32[]{:S(2)}) copy-start(f32[256,1408]{1,0:T(8,128)} %get-tuple-element.17) | copy-start | bytes 4325380

commit v2 on v1

v2 whole, which is shorter than its diff:
```python
import functools

import jax
import jax.numpy as jnp
from jax import lax
from jax.experimental import pallas as pl
from jax.experimental.pallas import tpu as pltpu
from jax.sharding import PartitionSpec as P

EXPERTS = 64
WAVE = 1
MOST = 48
F32 = jnp.float32
BF16 = jnp.bfloat16


def dot(a, b, dims):
    return lax.dot_general(a, b, (dims, ((), ())), preferred_element_type=F32)


MESH = pl.DeviceIdType.MESH
HBM = pl.BlockSpec(memory_space=pltpu.MemorySpace.HBM)
VMEM = pl.BlockSpec(memory_space=pltpu.MemorySpace.VMEM)


class Place:
    def __init__(self, groups):
        self.groups = groups
        self.e = lax.axis_index("expert")
        f = lax.axis_index("fsdp")
        self.f = f
        self.core = f % 2
        self.x, self.y = (f // 2) % 2, f // 4
        self.pair = f + 1 - 2 * self.core
        self.to_x, self.to_y = f + 2 - 4 * self.x, f + 4 - 8 * self.y

    def barrier(self):
        sem = pltpu.get_barrier_semaphore()
        peers = [(self.e, self.pair)]
        for step in range(self.groups):
            there = (self.e + step) % self.groups
            peers += [(there, self.to_x), (there, self.to_y)]
            if step:
                peers.append((there, self.f))
        for peer in peers:
            pl.semaphore_signal(sem, inc=1, device_id=peer, device_id_type=MESH)
        pl.semaphore_wait(sem, len(peers))


class Copies:
    def __init__(self, send, recv, local):
        self.sems = send, recv, local
        self.remote = self.near = 0
        self.pending = []

    def send(self, src, dst, to):
        send, recv, _ = self.sems
        copy = pltpu.make_async_remote_copy(
            src_ref=src,
            dst_ref=dst,
            send_sem=send.at[self.remote],
            recv_sem=recv.at[self.remote],
            device_id=to,
            device_id_type=MESH,
        )
        self.remote += 1
        copy.start()
        self.pending.append(copy)
        return copy

    def drain(self, copies):
        ids = {id(copy) for copy in copies}
        for copy in self.pending:
            if id(copy) in ids:
                copy.wait_send()
        self.pending = [copy for copy in self.pending if id(copy) not in ids]

    def keep(self, src, dst):
        copy = pltpu.make_async_copy(src, dst, self.sems[2].at[self.near])
        self.near += 1
        copy.start()
        return copy


GATE, UP, DOWN = range(3)
REMOTE = 128
LOCAL = 16


def chunks(ff):
    lanes = 128
    first = (ff // lanes + 1) // 2 * lanes
    return [pl.ds(0, first), pl.ds(first, ff - first)]


def route(groups, ids, gates):
    tok = ids.shape[1]
    rows = groups * MOST
    per_index = EXPERTS // groups
    slot = lax.broadcasted_iota(jnp.int32, (rows, tok), 0)
    target, place_in = jnp.zeros_like(slot), slot
    for g in range(1, groups):
        later = slot >= g * MOST
        target = target + jnp.where(later, per_index, 0)
        place_in = place_in - jnp.where(later, MOST, 0)
    chosen, gate_of = None, None
    vals = gates[...].astype(F32)
    for k in range(ids.shape[0]):
        hit = ids[pl.ds(k, 1), :] == target
        val = jnp.where(hit, vals[k : k + 1, :], 0.0)
        one = jnp.where(hit, 1.0, 0.0)
        chosen = one if chosen is None else chosen + one
        gate_of = val if gate_of is None else gate_of + val
    earlier = lax.broadcasted_iota(jnp.int32, (tok, tok), 0) < lax.broadcasted_iota(
        jnp.int32, (tok, tok), 1
    )
    rank = dot(chosen.astype(BF16), jnp.where(earlier, 1.0, 0.0).astype(BF16), ((1,), (0,)))
    place = (chosen > 0.0) & (rank == place_in.astype(F32))
    return (
        target,
        jnp.where(place, 1.0, 0.0).astype(BF16),
        jnp.where(place, gate_of, 0.0).astype(BF16),
    )


def layer_kernel(groups, *refs):
    ws, arrays_in = refs[:3], refs[3:7]
    owns, output, grad_tokens, grad_gates = refs[7:10], refs[10], refs[11], refs[12]
    full, xs, rows_in, acc, pre_out, pre_in, act = refs[13:20]
    pair_out, pair_in, near_in, back_in = refs[20:24]
    ids, gates, tokens, cotangent, pick, weighted = arrays = refs[24:30]
    at, go = Place(groups), Copies(*refs[30:33])
    block, ff = ws[0].shape
    rows = groups * MOST
    half_d = 4 * block
    cuts = chunks(ff)
    pair = (at.e, at.pair)
    across = [(at.e, at.to_y), (at.e, at.to_y), (at.e, at.to_x)]
    beside = [(at.e, at.to_x), (at.e, at.to_x), (at.e, at.to_y)]
    spot = [at.y, at.y, at.x]
    shape = (groups, MOST)
    first = ((0,), (0,))
    plain, turned = ((1,), (0,)), ((1,), (1,))
    top, low = pl.ds(0, rows), pl.ds(rows, rows)

    def span(q, s):
        return pl.ds(pl.multiple_of((2 * q + s) * block, block), block)

    def chip_span(q):
        return pl.ds(pl.multiple_of(2 * q * block, 2 * block), 2 * block)

    def fetch(m, c):
        return go.send(ws[m].at[:, c], full.at[m, span(spot[m], at.core), c], across[m])

    def near(m, c):
        where = full.at[m, span(spot[m], at.core), c]
        return [go.send(ws[m].at[:, c], where, pair), go.keep(ws[m].at[:, c], where)]

    def forward(m, c, copy):
        copy.wait_recv()
        where = full.at[m, span(1 - spot[m], at.core), c]
        return go.send(where, where, pair)

    def spread(src, dst, other, half):
        copies = []
        for step in range(groups):
            there = (at.e + step) % groups
            if half == 0 and step == 0:
                copies.append(go.keep(src.at[0, at.e], dst.at[0, at.e]))
            else:
                to = (there, other if half else at.f)
                copies.append(go.send(src.at[half, there], dst.at[half, at.e], to))
        return copies

    def wait_in(copies):
        for copy in copies:
            if copy.is_remote:
                copy.wait_recv()
            else:
                copy.wait()

    def x_cols(half, k):
        x = 1 - at.x if half else at.x
        return pl.ds(pl.multiple_of((4 * k + 2 * x) * block, 2 * block), 2 * block)

    def y_cols(half):
        y = 1 - at.y if half else at.y
        return pl.ds(pl.multiple_of(4 * y * block, half_d), half_d)

    loads = [go.keep(src, dst) for src, dst in zip(arrays_in, arrays)]
    at.barrier()
    coming = {}
    nearby = {}
    for m in (GATE, UP):
        coming[m, 0] = fetch(m, cuts[0])
    for m in (GATE, UP):
        nearby[m, 0] = near(m, cuts[0])
    wait_in(loads[:2])
    target, pick_val, weighted_val = route(groups, ids, gates)
    pick[...] = pick_val
    weighted[...] = weighted_val
    loads[2].wait()
    x_rows, og_rows = [], []
    for half in (1, 0):
        for k in range(2):
            val = dot(pick[...], tokens[:, x_cols(half, k)], plain).astype(BF16)
            xs[0, half, :, :, pl.ds(2 * k * block, 2 * block)] = val.reshape(shape + (2 * block,))
        x_rows += spread(xs.at[0], rows_in.at[0], at.to_x, half)
    for c in range(2):
        coming[DOWN, c] = fetch(DOWN, cuts[c])
    loads[3].wait()
    for half in (1, 0):
        val = dot(weighted[...], cotangent[:, y_cols(half)], plain).astype(BF16)
        xs[1, half] = val.reshape(shape + (half_d,))
        og_rows += spread(xs.at[1], rows_in.at[1], at.to_y, half)
    for m in (GATE, UP):
        coming[m, 1] = fetch(m, cuts[1])
    for m, c in ((DOWN, 0), (DOWN, 1), (GATE, 1), (UP, 1)):
        nearby[m, c] = near(m, cuts[c])

    def lhs(t, cols):
        return rows_in[t, :, :, :, cols].reshape(2 * rows, -1)

    def begin(m, t, c):
        wait_in(nearby[m, c])
        cut, where = cuts[c], chip_span(spot[m])
        acc[m, :, cut] = dot(lhs(t, where), full[m, where, cut], plain)

    def finish(m, t, c, far):
        far.wait_recv()
        cut, where = cuts[c], chip_span(1 - spot[m])
        acc[m, :, cut] += dot(lhs(t, where), full[m, where, cut], plain)
        pre_out[m, top, cut] = acc[m, low, cut].astype(BF16)
        return go.send(pre_out.at[m, top, cut], pre_in.at[m, :, cut], beside[m])

    tile = 16

    def make_hidden(c):
        cut = cuts[c]

        def body(i, _):
            r = pl.ds(pl.multiple_of(i * tile, tile), tile)
            g = acc[GATE, r, cut] + pre_in[GATE, r, cut].astype(F32)
            u = acc[UP, r, cut] + pre_in[UP, r, cut].astype(F32)
            acc[GATE, r, cut] = g
            acc[UP, r, cut] = u
            act[DOWN, r, cut] = (g * jax.nn.sigmoid(g) * u).astype(BF16)
            return 0

        lax.fori_loop(0, rows // tile, body, 0)

    def make_grads(c):
        cut = cuts[c]

        def body(i, _):
            r = pl.ds(pl.multiple_of(i * tile, tile), tile)
            g, u = acc[GATE, r, cut], acc[UP, r, cut]
            h = acc[DOWN, r, cut] + pre_in[DOWN, r, cut].astype(F32)
            s = jax.nn.sigmoid(g)
            act[GATE, r, cut] = (h * u * s * (1.0 + g * (1.0 - s))).astype(BF16)
            act[UP, r, cut] = (h * g * s).astype(BF16)
            return 0

        lax.fori_loop(0, rows // tile, body, 0)

    def share(m, c):
        return go.send(act.at[m, top, cuts[c]], act.at[m, low, cuts[c]], beside[m])

    ends = []
    back_out = xs

    def grads(m, t, c):
        cut, q, other = cuts[c], spot[m], 1 - spot[m]

        def term(q, s):
            return dot(lhs(t, span(q, s)), act[m, :, cut], first)

        pair_out[m, 0, :, cut] = term(other, 1 - at.core).astype(BF16)
        to_far = go.send(pair_out.at[m, 0, :, cut], pair_in.at[m, 0, :, cut], pair)
        acc[m, pl.ds(0, block), cut] = term(other, at.core)
        pair_out[m, 1, :, cut] = term(q, 1 - at.core).astype(BF16)
        to_pair = go.send(pair_out.at[m, 1, :, cut], pair_in.at[m, 1, :, cut], pair)
        to_far.wait_recv()
        both = acc[m, pl.ds(0, block), cut] + pair_in[m, 0, :, cut].astype(F32)
        pre_out[m, :, cut] = both.astype(BF16)
        to_other = go.send(pre_out.at[m, :, cut], near_in.at[m, :, cut], across[m])
        owns[m][:, cut] = term(q, at.core)
        ends.append((m, c, to_other, to_pair))

    pre, got = {}, {}
    far = {(m, 0): forward(m, cuts[0], coming[m, 0]) for m in (GATE, UP)}
    wait_in(x_rows)
    for m in (GATE, UP):
        begin(m, 0, 0)
    for m in (GATE, UP):
        pre[m, 0] = finish(m, 0, 0, far[m, 0])
    for c in range(2):
        far[DOWN, c] = forward(DOWN, cuts[c], coming[DOWN, c])
    for m in (GATE, UP):
        begin(m, 0, 1)
    far[GATE, 1] = forward(GATE, cuts[1], coming[GATE, 1])
    wait_in(og_rows)
    for c in range(2):
        begin(DOWN, 1, c)
        pre[DOWN, c] = finish(DOWN, 1, c, far[DOWN, c])
    pre[GATE, 0].wait_recv()
    pre[UP, 0].wait_recv()
    make_hidden(0)
    got[DOWN, 0] = share(DOWN, 0)
    pre[GATE, 1] = finish(GATE, 0, 1, far[GATE, 1])
    far[UP, 1] = forward(UP, cuts[1], coming[UP, 1])
    pre[UP, 1] = finish(UP, 0, 1, far[UP, 1])
    pre[DOWN, 0].wait_recv()
    make_grads(0)
    for m in (GATE, UP):
        got[m, 0] = share(m, 0)
    pre[GATE, 1].wait_recv()
    pre[UP, 1].wait_recv()
    make_hidden(1)
    got[DOWN, 1] = share(DOWN, 1)
    pre[DOWN, 1].wait_recv()
    make_grads(1)
    for m in (GATE, UP):
        got[m, 1] = share(m, 1)

    go.drain(list(pre.values()) + x_rows + og_rows)
    got[GATE, 0].wait_recv()
    grads(GATE, 0, 0)
    got[DOWN, 0].wait_recv()
    got[DOWN, 1].wait_recv()
    back_out[0] = dot(act[DOWN], full[DOWN], turned).astype(BF16).reshape((2,) + shape + (half_d,))
    back, back_grad = [], []
    for half in (1, 0):
        back += spread(back_out.at[0], back_in.at[0], at.to_y, half)
    got[UP, 0].wait_recv()
    grads(UP, 0, 0)
    grads(DOWN, 1, 0)
    got[GATE, 1].wait_recv()
    got[UP, 1].wait_recv()
    slot_grad = dot(act[GATE], full[GATE], turned) + dot(act[UP], full[UP], turned)
    back_out[1] = slot_grad.astype(BF16).reshape((2,) + shape + (half_d,))
    for half in (1, 0):
        back_grad += spread(back_out.at[1], back_in.at[1], at.to_x, half)
    grads(GATE, 0, 1)
    grads(UP, 0, 1)
    grads(DOWN, 1, 1)

    wait_in(back)
    met = None
    for half in range(2):
        slot = back_in[0, half].reshape(rows, half_d)
        output[:, y_cols(half)] = dot(weighted[...], slot, first).astype(BF16)
        val = dot(slot, cotangent[:, y_cols(half)], turned)
        met = val if met is None else met + val
    met = jnp.where(pick[...].astype(F32) > 0.0, met, 0.0)
    for k in range(ids.shape[0]):
        hit = jnp.where(ids[pl.ds(k, 1), :] == target, met, 0.0)
        grad_gates[pl.ds(k, 1), :] = jnp.sum(hit, axis=0, keepdims=True)
    wait_in(back_grad)
    for half in range(2):
        for k in range(2):
            slot = back_in[1, half, :, :, pl.ds(2 * k * block, 2 * block)].reshape(rows, 2 * block)
            grad_tokens[:, x_cols(half, k)] = dot(pick[...], slot, first).astype(BF16)
    for m, c, to_other, to_pair in ends:
        cut = cuts[c]
        to_pair.wait_recv()
        to_other.wait_recv()
        owns[m][:, cut] += pair_in[m, 1, :, cut].astype(F32) + near_in[m, :, cut].astype(F32)
    go.drain(go.pending)


def stay(x):
    return pltpu.with_memory_space_constraint(x, pltpu.MemorySpace.HBM)


def layer_call(groups, ws, ids, gates, tokens, cotangent):
    dma = pltpu.SemaphoreType.DMA
    block, ff = ws[0].shape
    tok, width = tokens.shape
    rows = groups * MOST
    wide = (2, 2, groups, MOST, width // 2)
    vmem = pltpu.VMEM
    return pl.pallas_call(
        functools.partial(layer_kernel, groups),
        out_shape=[jax.ShapeDtypeStruct((block, ff), F32)] * 3
        + [jax.ShapeDtypeStruct((tok, width), BF16)] * 2
        + [jax.ShapeDtypeStruct(ids.shape, F32)],
        in_specs=[HBM] * 7,
        out_specs=[VMEM] * 6,
        scratch_shapes=[
            vmem((3, 4 * block, ff), BF16),
            vmem(wide, BF16),
            vmem(wide, BF16),
            vmem((3, 2 * rows, ff), F32),
            vmem((3, block, ff), BF16),
            vmem((3, rows, ff), BF16),
            vmem((3, 2 * rows, ff), BF16),
            vmem((3, 2, block, ff), BF16),
            vmem((3, 2, block, ff), BF16),
            vmem((3, block, ff), BF16),
            vmem(wide, BF16),
            vmem(ids.shape, ids.dtype),
            vmem(gates.shape, gates.dtype),
            vmem((tok, width), BF16),
            vmem((tok, width), BF16),
            vmem((rows, tok), BF16),
            vmem((rows, tok), BF16),
            dma((REMOTE,)),
            dma((REMOTE,)),
            dma((LOCAL,)),
        ],
        compiler_params=pltpu.CompilerParams(
            collective_id=0, has_side_effects=True, vmem_limit_bytes=41 * 2**20
        ),
    )(*map(stay, [*ws, ids, gates, tokens, cotangent]))


def store_kernel(*refs):
    n = len(refs) // 2
    srcs, dsts, sems = refs[:n], refs[n : 2 * n], refs[2 * n]
    copies = [pltpu.make_async_copy(srcs[i], dsts[i], sems.at[i]) for i in range(n)]
    for copy in copies:
        copy.start()
    for copy in copies:
        copy.wait()


def store_call(arrays):
    return pl.pallas_call(
        store_kernel,
        out_shape=[jax.ShapeDtypeStruct(a.shape, a.dtype) for a in arrays],
        in_specs=[VMEM] * len(arrays),
        out_specs=[HBM] * len(arrays),
        scratch_shapes=[pltpu.SemaphoreType.DMA((len(arrays),))],
        compiler_params=pltpu.CompilerParams(vmem_limit_bytes=2**20),
    )(*arrays)


def routes(expert_ids, gate_vals, groups):
    per_index = EXPERTS // groups
    window = WAVE * groups
    tok_count = expert_ids.shape[0]
    local_index = expert_ids % per_index
    window_slot = jnp.where(
        local_index < WAVE, expert_ids // per_index * WAVE + local_index, window
    )
    slot_is = window_slot[:, :, None] == jnp.arange(window, dtype=jnp.int32)[None, None, :]
    chosen = jnp.any(slot_is, axis=1)
    gate_of = jnp.sum(jnp.where(slot_is, gate_vals.astype(F32)[:, :, None], 0.0), axis=1)
    tok = jnp.arange(tok_count, dtype=jnp.int32)
    before = (tok[:, None] > tok[None, :]).astype(BF16)
    rank = dot(before, chosen.astype(BF16), ((1,), (0,))).astype(jnp.int32)
    place = chosen[:, :, None] & (
        rank[:, :, None] == jnp.arange(MOST, dtype=jnp.int32)[None, None, :]
    )
    pick = place.astype(BF16).reshape(tok_count, window * MOST)
    weighted = (
        jnp.where(place, gate_of[:, :, None], 0.0).astype(BF16).reshape(tok_count, window * MOST)
    )
    return slot_is, place, pick, weighted


def on_device(tokens, expert_ids, gate_vals, w_gate, w_up, w_down, cotangent):
    groups = lax.axis_size("expert")
    columns = lax.axis_size("fsdp")
    side = lax.axis_index("fsdp") % 2
    tok_count, width = tokens.shape
    block = w_gate.shape[1]
    rows = groups * MOST
    sides = [[i for i in range(columns) if i % 2 == s] for s in (0, 1)]
    pairs = [(i, i ^ 1) for i in range(columns)]

    def swap(x):
        return lax.ppermute(x, "fsdp", pairs)

    def gather(w):
        return lax.all_gather(w[0], "fsdp", axis_index_groups=sides, axis=0, tiled=True)

    def scatter(x):
        return lax.psum_scatter(
            x.astype(BF16), "fsdp", scatter_dimension=0, axis_index_groups=sides, tiled=True
        ).astype(F32)[None]

    def cut(x, odd):
        return jnp.concatenate(
            [x[:, (2 * k + odd) * block : (2 * k + odd + 1) * block] for k in range(columns // 2)],
            axis=1,
        )

    def halves(x):
        even, odd = cut(x, 0), cut(x, 1)
        return jnp.where(side == 0, even, odd), jnp.where(side == 0, odd, even)

    def whole_rows(mine, other):
        even, odd = jnp.where(side == 0, mine, other), jnp.where(side == 0, other, mine)
        parts = []
        for k in range(columns // 2):
            here = slice(k * block, (k + 1) * block)
            parts += [even[:, here], odd[:, here]]
        return jnp.concatenate(parts, axis=1)

    def exchange(mine, other):
        packed = jnp.stack(
            [mine.reshape(groups, MOST, width // 2), other.reshape(groups, MOST, width // 2)],
            axis=1,
        )
        there = lax.all_to_all(packed, "expert", split_axis=0, concat_axis=0, tiled=True)
        return there[:, 0].reshape(rows, width // 2), there[:, 1].reshape(rows, width // 2)

    square = columns == 8
    first = ((0,), (0,))
    if square:
        results = layer_call(
            groups, [w_gate[0], w_up[0], w_down[0]], expert_ids.T, gate_vals.T, tokens, cotangent
        )
        *grad_w, output, grad_tokens, grad_gates = store_call(results)
        return (output, grad_tokens, grad_gates.T, *(g[None] for g in grad_w))
    slot_is, place, pick, weighted = routes(expert_ids, gate_vals, groups)
    full_gate, full_up, full_down = gather(w_gate), gather(w_up), gather(w_down)
    row_mine, row_other = exchange(*halves(dot(pick, tokens, first).astype(BF16)))
    og_mine, og_other = exchange(*halves(dot(weighted, cotangent, first).astype(BF16)))
    row_in = jnp.concatenate([row_mine, swap(row_other)], axis=0)
    out_grad = jnp.concatenate([og_mine, swap(og_other)], axis=0)

    def summed(x):
        return x[:rows] + swap(x[rows:].astype(BF16)).astype(F32)

    def both(x):
        return jnp.concatenate([x, swap(x)], axis=0)

    plain, turned = ((1,), (0,)), ((1,), (1,))
    gate_pre = summed(dot(row_in, full_gate, plain))
    up_pre = summed(dot(row_in, full_up, plain))
    sigmoid_g = jax.nn.sigmoid(gate_pre)
    hidden = (gate_pre * sigmoid_g * up_pre).astype(BF16)
    hidden_grad = summed(dot(out_grad, full_down, plain))
    gate_grad = (
        hidden_grad * up_pre * sigmoid_g * (1.0 + gate_pre * (1.0 - sigmoid_g))
    ).astype(BF16)
    up_grad = (hidden_grad * gate_pre * sigmoid_g).astype(BF16)
    hidden, gate_grad, up_grad = both(hidden), both(gate_grad), both(up_grad)
    grad_w_down = scatter(dot(out_grad, hidden, first))
    grad_w_gate = scatter(dot(row_in, gate_grad, first))
    grad_w_up = scatter(dot(row_in, up_grad, first))
    expert_out = dot(hidden, full_down, turned).astype(BF16)
    slot_grad = (dot(gate_grad, full_gate, turned) + dot(up_grad, full_up, turned)).astype(BF16)
    outs = exchange(expert_out[:rows], swap(expert_out[rows:]))
    grads = exchange(slot_grad[:rows], swap(slot_grad[rows:]))

    slot_out = whole_rows(*outs)
    output = dot(weighted, slot_out, plain).astype(BF16)
    grad_tokens = dot(pick, whole_rows(*grads), plain).astype(BF16)
    met = dot(cotangent, slot_out, turned)
    met = jnp.sum(jnp.where(place, met.reshape(place.shape), 0.0), axis=2)
    grad_gates = jnp.sum(jnp.where(slot_is, met[:, None, :], 0.0), axis=2)
    return (output, grad_tokens, grad_gates, grad_w_gate, grad_w_up, grad_w_down)


def solution(mesh):
    token = P(("expert", "fsdp"), None)
    weight = P("expert", "fsdp", None)
    return jax.shard_map(
        on_device,
        mesh=mesh,
        in_specs=(token, token, token, weight, weight, weight, token),
        out_specs=(token, token, token, weight, weight, weight),
        check_vma=False,
    )
```

time: 140 us -> 117 us (0.84)
  local copies, waits for them, and re-layouts: 10.6 us -> 0 us
  Pallas kernels: 125 us -> 115 us
  other arithmetic: 3.56 us -> 0 us
    pallas_call x1, Pallas kernels: 125 us -> 113 us  [layer_call(): pl.pallas_call(functools.partial(layer_kernel, groups), out_shape=[jax.Sh...]
    unnamed x13 -> x0, local copies, waits for them, and re-layouts: 8.91 us -> none
    pallas_call x0 -> x1, Pallas kernels: none -> 2.77 us  [store_call(): pl.pallas_call(store_kernel, out_shape=[jax.ShapeDtypeStruct(a.shape, a.d...]
    convert_element_type x3 -> x0, other arithmetic: 2.13 us -> none  [the longest x1 0.74 us: routes(): jnp.where(place, gate_of[:, :, None], 0.0).astype(BF16)]
where the time goes in v2:
time: 117 us; the launch traced here: 116 us
  Pallas kernels  115 us (98%)
    pallas_call x1, Pallas kernels, layer_call(): pl.pallas_call(functools.partial(layer_kernel, groups), out_shape=[jax.Sh...  113 us
    pallas_call x1, Pallas kernels, store_call(): pl.pallas_call(store_kernel, out_shape=[jax.ShapeDtypeStruct(a.shape, a.d...  2.77 us

profile of v2, /device:TPU:0, one launch (start us, length us, event | category | flops | bytes accessed | tf_op | source)
XLA Modules:
  0.0 116.3 jit_solution(1869393979208249403)
XLA Ops:
  0.6 112.7 %shard_map.118 = (f32[256,1408]{1,0:T(8,128)S(1)}, f32[256,1408]{1,0:T(8,128)S(1)}, f32[256,1408]{1,0:T(8,128)S(1)}, bf16[256,2048]{1,0:T(8,128)(2,1)S(1)}, bf16...) custom-call(bf16[256,1408]{1,0:T(8,128)(2,1)} %bitcast.9, bf16[256,1408]{1,0:T(8,128)(2,1)} %bitcast.10, ...), custom_call_target="tpu_custom_call" | custom-call | tf_op jit(solution)/shard_map/pallas_call | solution.py:383
  113.4 2.8 %shard_map.119 = (f32[256,1408]{1,0:T(8,128)}, f32[256,1408]{1,0:T(8,128)}, f32[256,1408]{1,0:T(8,128)}, bf16[256,2048]{1,0:T(8,128)(2,1)}, bf16[256,2048]{1,0:T(8,128)(2,1)}, /*index=5*/f32[6,256]{1,0:T(8,128)}) custom-call(f32[256,1408]{1,0:T(8,128)S(1)} %get-tuple-element.18.refs_0_, f32[256,1408]{1,0:T(8,128)S(1)} %get-tuple-element.19.refs_1_, ...), custom_call_target="tpu_custom_call" | custom-call | tf_op jit(solution)/shard_map/pallas_call | solution.py:429

commit v3 on v2

--- a/solution.py
+++ b/solution.py
@@ -32,19 +32,44 @@
         self.core = f % 2
         self.x, self.y = (f // 2) % 2, f // 4
         self.pair = f + 1 - 2 * self.core
+        self.others = [3 - self.e, (self.e + 2) % 4, self.e + 1 - 2 * (self.e % 2)]
         self.to_x, self.to_y = f + 2 - 4 * self.x, f + 4 - 8 * self.y
 
-    def barrier(self):
+    def planes(self):
+        return [(1, self.others[2]), (3, self.others[0]), (2, self.others[1]), (0, self.e)]
+
+    def tell(self, sem, e, f):
+        pl.semaphore_signal(sem, inc=1, device_id=(e, f), device_id_type=MESH)
+
+    def enter_plane(self, plane_sem):
         sem = pltpu.get_barrier_semaphore()
-        peers = [(self.e, self.pair)]
-        for step in range(self.groups):
-            there = (self.e + step) % self.groups
-            peers += [(there, self.to_x), (there, self.to_y)]
-            if step:
-                peers.append((there, self.f))
-        for peer in peers:
-            pl.semaphore_signal(sem, inc=1, device_id=peer, device_id_type=MESH)
-        pl.semaphore_wait(sem, len(peers))
+        self.tell(sem, self.e, self.to_x - self.core)
+        self.tell(sem, self.e, self.to_y - self.core)
+
+        @pl.when(self.core == 1)
+        def _():
+            self.tell(sem, self.e, self.pair)
+
+        @pl.when(self.core == 0)
+        def _():
+            pl.semaphore_wait(sem, 5)
+            self.tell(plane_sem, self.e, self.pair)
+
+        @pl.when(self.core == 1)
+        def _():
+            pl.semaphore_wait(plane_sem, 1)
+            for there in self.others:
+                self.tell(sem, there, self.f)
+
+    def enter_slice(self, slice_sem):
+        @pl.when(self.core == 1)
+        def _():
+            pl.semaphore_wait(pltpu.get_barrier_semaphore(), self.groups - 1)
+            self.tell(slice_sem, self.e, self.pair)
+
+        @pl.when(self.core == 0)
+        def _():
+            pl.semaphore_wait(slice_sem, 1)
 
 
 class Copies:
@@ -163,8 +188,7 @@
 
     def spread(src, dst, other, half):
         copies = []
-        for step in range(groups):
-            there = (at.e + step) % groups
+        for step, there in at.planes():
             if half == 0 and step == 0:
                 copies.append(go.keep(src.at[0, at.e], dst.at[0, at.e]))
             else:
@@ -188,11 +212,13 @@
         return pl.ds(pl.multiple_of(4 * y * block, half_d), half_d)
 
     loads = [go.keep(src, dst) for src, dst in zip(arrays_in, arrays)]
-    at.barrier()
+    plane_sem, slice_sem = refs[33:35]
+    at.enter_plane(plane_sem)
     coming = {}
     nearby = {}
     for m in (GATE, UP):
         coming[m, 0] = fetch(m, cuts[0])
+    coming[DOWN, 0] = fetch(DOWN, cuts[0])
     for m in (GATE, UP):
         nearby[m, 0] = near(m, cuts[0])
     wait_in(loads[:2])
@@ -205,13 +231,16 @@
         for k in range(2):
             val = dot(pick[...], tokens[:, x_cols(half, k)], plain).astype(BF16)
             xs[0, half, :, :, pl.ds(2 * k * block, 2 * block)] = val.reshape(shape + (2 * block,))
+    at.enter_slice(slice_sem)
+    for half in (1, 0):
         x_rows += spread(xs.at[0], rows_in.at[0], at.to_x, half)
-    for c in range(2):
-        coming[DOWN, c] = fetch(DOWN, cuts[c])
     loads[3].wait()
     for half in (1, 0):
         val = dot(weighted[...], cotangent[:, y_cols(half)], plain).astype(BF16)
         xs[1, half] = val.reshape(shape + (half_d,))
+    far = {(GATE, 0): forward(GATE, cuts[0], coming[GATE, 0])}
+    coming[DOWN, 1] = fetch(DOWN, cuts[1])
+    for half in (1, 0):
         og_rows += spread(xs.at[1], rows_in.at[1], at.to_y, half)
     for m in (GATE, UP):
         coming[m, 1] = fetch(m, cuts[1])
@@ -287,8 +316,22 @@
         owns[m][:, cut] = term(q, at.core)
         ends.append((m, c, to_other, to_pair))
 
+    back, back_grad = [], []
+
+    def send_out(half):
+        r = low if half else top
+        val = dot(act[DOWN, r], full[DOWN], turned)
+        back_out[0, half] = val.astype(BF16).reshape(shape + (half_d,))
+        back.extend(spread(back_out.at[0], back_in.at[0], at.to_y, half))
+
+    def send_grad(half):
+        r = low if half else top
+        val = dot(act[GATE, r], full[GATE], turned) + dot(act[UP, r], full[UP], turned)
+        back_out[1, half] = val.astype(BF16).reshape(shape + (half_d,))
+        back_grad.extend(spread(back_out.at[1], back_in.at[1], at.to_x, half))
+
     pre, got = {}, {}
-    far = {(m, 0): forward(m, cuts[0], coming[m, 0]) for m in (GATE, UP)}
+    far[UP, 0] = forward(UP, cuts[0], coming[UP, 0])
     wait_in(x_rows)
     for m in (GATE, UP):
         begin(m, 0, 0)
@@ -318,29 +361,26 @@
     pre[UP, 1].wait_recv()
     make_hidden(1)
     got[DOWN, 1] = share(DOWN, 1)
+    go.drain(x_rows + og_rows)
+    send_out(0)
     pre[DOWN, 1].wait_recv()
     make_grads(1)
     for m in (GATE, UP):
         got[m, 1] = share(m, 1)
-
-    go.drain(list(pre.values()) + x_rows + og_rows)
+    send_grad(0)
+
+    go.drain(list(pre.values()))
     got[GATE, 0].wait_recv()
     grads(GATE, 0, 0)
     got[DOWN, 0].wait_recv()
     got[DOWN, 1].wait_recv()
-    back_out[0] = dot(act[DOWN], full[DOWN], turned).astype(BF16).reshape((2,) + shape + (half_d,))
-    back, back_grad = [], []
-    for half in (1, 0):
-        back += spread(back_out.at[0], back_in.at[0], at.to_y, half)
+    send_out(1)
     got[UP, 0].wait_recv()
     grads(UP, 0, 0)
     grads(DOWN, 1, 0)
     got[GATE, 1].wait_recv()
     got[UP, 1].wait_recv()
-    slot_grad = dot(act[GATE], full[GATE], turned) + dot(act[UP], full[UP], turned)
-    back_out[1] = slot_grad.astype(BF16).reshape((2,) + shape + (half_d,))
-    for half in (1, 0):
-        back_grad += spread(back_out.at[1], back_in.at[1], at.to_x, half)
+    send_grad(1)
     grads(GATE, 0, 1)
     grads(UP, 0, 1)
     grads(DOWN, 1, 1)
@@ -408,6 +448,8 @@
             dma((REMOTE,)),
             dma((REMOTE,)),
             dma((LOCAL,)),
+            pltpu.SemaphoreType.REGULAR,
+            pltpu.SemaphoreType.REGULAR,
         ],
         compiler_params=pltpu.CompilerParams(
             collective_id=0, has_side_effects=True, vmem_limit_bytes=41 * 2**20
@@ -507,7 +549,7 @@
         there = lax.all_to_all(packed, "expert", split_axis=0, concat_axis=0, tiled=True)
         return there[:, 0].reshape(rows, width // 2), there[:, 1].reshape(rows, width // 2)
 
-    square = columns == 8
+    square = columns == 8 and groups == 4
     first = ((0,), (0,))
     if square:
         results = layer_call(

time: 117 us -> 114 us (0.974)
  Pallas kernels: 115 us -> 113 us
    pallas_call x1, Pallas kernels: 113 us -> 111 us  [layer_call(): pl.pallas_call(functools.partial(layer_kernel, groups), out_shape=[jax.Sh...]
where the time goes in v3:
time: 114 us
  Pallas kernels  113 us (99%)
    pallas_call x1, Pallas kernels, layer_call(): pl.pallas_call(functools.partial(layer_kernel, groups), out_shape=[jax.Sh...  111 us
    pallas_call x1, Pallas kernels, store_call(): pl.pallas_call(store_kernel, out_shape=[jax.ShapeDtypeStruct(a.shape, a.d...  2.77 us

profile of v3, /device:TPU:0, one launch (start us, length us, event | category | flops | bytes accessed | tf_op | source)
XLA Modules:
  0.0 114.2 jit_solution(15787260106789068555)
XLA Ops:
  0.6 110.6 %shard_map.118 = (f32[256,1408]{1,0:T(8,128)S(1)}, f32[256,1408]{1,0:T(8,128)S(1)}, f32[256,1408]{1,0:T(8,128)S(1)}, bf16[256,2048]{1,0:T(8,128)(2,1)S(1)}, bf16...) custom-call(bf16[256,1408]{1,0:T(8,128)(2,1)} %bitcast.9, bf16[256,1408]{1,0:T(8,128)(2,1)} %bitcast.10, ...), custom_call_target="tpu_custom_call" | custom-call | tf_op jit(solution)/shard_map/pallas_call | solution.py:423
  111.3 2.8 %shard_map.119 = (f32[256,1408]{1,0:T(8,128)}, f32[256,1408]{1,0:T(8,128)}, f32[256,1408]{1,0:T(8,128)}, bf16[256,2048]{1,0:T(8,128)(2,1)}, bf16[256,2048]{1,0:T(8,128)(2,1)}, /*index=5*/f32[6,256]{1,0:T(8,128)}) custom-call(f32[256,1408]{1,0:T(8,128)S(1)} %get-tuple-element.18.refs_0_, f32[256,1408]{1,0:T(8,128)S(1)} %get-tuple-element.19.refs_1_, ...), custom_call_target="tpu_custom_call" | custom-call | tf_op jit(solution)/shard_map/pallas_call | solution.py:471

commit v4 on v3

--- a/solution.py
+++ b/solution.py
@@ -75,15 +75,20 @@
 class Copies:
     def __init__(self, send, recv, local):
         self.sems = send, recv, local
-        self.remote = self.near = 0
+        self.remote = self.near = self.sending = 0
+        self.free, self.slot = [], {}
         self.pending = []
 
     def send(self, src, dst, to):
         send, recv, _ = self.sems
+        if self.free:
+            slot = self.free.pop()
+        else:
+            slot, self.sending = self.sending, self.sending + 1
         copy = pltpu.make_async_remote_copy(
             src_ref=src,
             dst_ref=dst,
-            send_sem=send.at[self.remote],
+            send_sem=send.at[slot],
             recv_sem=recv.at[self.remote],
             device_id=to,
             device_id_type=MESH,
@@ -91,6 +96,7 @@
         self.remote += 1
         copy.start()
         self.pending.append(copy)
+        self.slot[id(copy)] = slot
         return copy
 
     def drain(self, copies):
@@ -98,6 +104,7 @@
         for copy in self.pending:
             if id(copy) in ids:
                 copy.wait_send()
+                self.free.append(self.slot[id(copy)])
         self.pending = [copy for copy in self.pending if id(copy) not in ids]
 
     def keep(self, src, dst):
@@ -108,8 +115,9 @@
 
 
 GATE, UP, DOWN = range(3)
-REMOTE = 128
-LOCAL = 16
+SENDS = 56
+REMOTE = 76
+LOCAL = 14
 
 
 def chunks(ff):
@@ -407,6 +415,7 @@
         to_other.wait_recv()
         owns[m][:, cut] += pair_in[m, 1, :, cut].astype(F32) + near_in[m, :, cut].astype(F32)
     go.drain(go.pending)
+    assert (go.sending, go.remote, go.near) == (SENDS, REMOTE, LOCAL)
 
 
 def stay(x):
@@ -445,7 +454,7 @@
             vmem((tok, width), BF16),
             vmem((rows, tok), BF16),
             vmem((rows, tok), BF16),
-            dma((REMOTE,)),
+            dma((SENDS,)),
             dma((REMOTE,)),
             dma((LOCAL,)),
             pltpu.SemaphoreType.REGULAR,

time: 114 us -> 113 us (level)
  no operation moved by 1% of the time
where the time goes in v4:
time: 113 us
  Pallas kernels  112 us (99%)
    pallas_call x1, Pallas kernels, layer_call(): pl.pallas_call(functools.partial(layer_kernel, groups), out_shape=[jax.Sh...  110 us
    pallas_call x1, Pallas kernels, store_call(): pl.pallas_call(store_kernel, out_shape=[jax.ShapeDtypeStruct(a.shape, a.d...  2.77 us

profile of v4, /device:TPU:0, one launch (start us, length us, event | category | flops | bytes accessed | tf_op | source)
XLA Modules:
  0.0 113.1 jit_solution(18025120009494851489)
XLA Ops:
  0.6 109.5 %shard_map.118 = (f32[256,1408]{1,0:T(8,128)S(1)}, f32[256,1408]{1,0:T(8,128)S(1)}, f32[256,1408]{1,0:T(8,128)S(1)}, bf16[256,2048]{1,0:T(8,128)(2,1)S(1)}, bf16...) custom-call(bf16[256,1408]{1,0:T(8,128)(2,1)} %bitcast.9, bf16[256,1408]{1,0:T(8,128)(2,1)} %bitcast.10, ...), custom_call_target="tpu_custom_call" | custom-call | tf_op jit(solution)/shard_map/pallas_call | solution.py:432
  110.1 2.8 %shard_map.119 = (f32[256,1408]{1,0:T(8,128)}, f32[256,1408]{1,0:T(8,128)}, f32[256,1408]{1,0:T(8,128)}, bf16[256,2048]{1,0:T(8,128)(2,1)}, bf16[256,2048]{1,0:T(8,128)(2,1)}, /*index=5*/f32[6,256]{1,0:T(8,128)}) custom-call(f32[256,1408]{1,0:T(8,128)S(1)} %get-tuple-element.18.refs_0_, f32[256,1408]{1,0:T(8,128)S(1)} %get-tuple-element.19.refs_1_, ...), custom_call_target="tpu_custom_call" | custom-call | tf_op jit(solution)/shard_map/pallas_call | solution.py:480

commit v5 on v4

--- a/solution.py
+++ b/solution.py
@@ -115,7 +115,7 @@
 
 
 GATE, UP, DOWN = range(3)
-SENDS = 56
+SENDS = 42
 REMOTE = 76
 LOCAL = 14
 
@@ -369,7 +369,8 @@
     pre[UP, 1].wait_recv()
     make_hidden(1)
     got[DOWN, 1] = share(DOWN, 1)
-    go.drain(x_rows + og_rows)
+    weights = list(coming.values()) + list(far.values()) + [pair_of[0] for pair_of in nearby.values()]
+    go.drain(x_rows + og_rows + weights)
     send_out(0)
     pre[DOWN, 1].wait_recv()
     make_grads(1)

time: 113 us -> 113 us (level)
  no operation moved by 1% of the time
where the time goes in v5:
time: 113 us
  Pallas kernels  112 us (99%)
    pallas_call x1, Pallas kernels, layer_call(): pl.pallas_call(functools.partial(layer_kernel, groups), out_shape=[jax.Sh...  109 us
    pallas_call x1, Pallas kernels, store_call(): pl.pallas_call(store_kernel, out_shape=[jax.ShapeDtypeStruct(a.shape, a.d...  2.77 us

profile of v5, /device:TPU:0, one launch (start us, length us, event | category | flops | bytes accessed | tf_op | source)
XLA Modules:
  0.0 112.9 jit_solution(18297547539035204009)
XLA Ops:
  0.6 109.4 %shard_map.118 = (f32[256,1408]{1,0:T(8,128)S(1)}, f32[256,1408]{1,0:T(8,128)S(1)}, f32[256,1408]{1,0:T(8,128)S(1)}, bf16[256,2048]{1,0:T(8,128)(2,1)S(1)}, bf16...) custom-call(bf16[256,1408]{1,0:T(8,128)(2,1)} %bitcast.9, bf16[256,1408]{1,0:T(8,128)(2,1)} %bitcast.10, ...), custom_call_target="tpu_custom_call" | custom-call | tf_op jit(solution)/shard_map/pallas_call | solution.py:433
  110.0 2.8 %shard_map.119 = (f32[256,1408]{1,0:T(8,128)}, f32[256,1408]{1,0:T(8,128)}, f32[256,1408]{1,0:T(8,128)}, bf16[256,2048]{1,0:T(8,128)(2,1)}, bf16[256,2048]{1,0:T(8,128)(2,1)}, /*index=5*/f32[6,256]{1,0:T(8,128)}) custom-call(f32[256,1408]{1,0:T(8,128)S(1)} %get-tuple-element.18.refs_0_, f32[256,1408]{1,0:T(8,128)S(1)} %get-tuple-element.19.refs_1_, ...), custom_call_target="tpu_custom_call" | custom-call | tf_op jit(solution)/shard_map/pallas_call | solution.py:481
